TPU v7x, 256 devices: a whole 4x4x8 slice. The times are simulated.
256 devices in a mesh: fsdp: 32 (over y, x, core), tp: 8 (over z).
Axes of the slice: x: 4, y: 4, z: 8, core: 2. Of those that a mesh axis runs over, the one named last changes fastest.
Arguments:
- learner_flat: bfloat16 [2, 159383552], P(None, ('fsdp', 'tp')), may hold values from -1.796875 to 1.796875
- param_offsets: int32 [2, 128, 4], replicated, may hold values from 0 to 622336, as said below
- owner_map: int32 [2, 128], replicated, may hold values from 0 to 31, as said below
- slice_map: int32 [32, 8], replicated, may hold values from 0 to 7, each once within a row
Outputs:
- query_absorbed: bfloat16 [2, 128, 1536, 512], P(None, 'fsdp', 'tp')
- output_absorbed: bfloat16 [2, 128, 7168, 512], P(None, 'fsdp', 'tp')
Inputs may be any that keep to these rules, and one draw needn't show every extreme that they name: `param_offsets`: in each layer the pieces of all heads' four parameters lie in a rank's 622592 entries one after another in some order, without gaps or intersections; a piece of a parameter holds that parameter's entries divided by 256; the last piece of each layer is a key up-projection piece. `owner_map`: in each layer every index of fsdp owns exactly 4 heads.
All inputs are finite; a program needn't handle non-finite values.
Results may differ from a plain program's by a relative error of at most 0.001.
Values may be sent and summed in bfloat16 or wider, within the bound.
A program may use at most 64 MiB of HBM per device.

v0:
```python
import math
import jax
import jax.numpy as jnp
from jax import lax
from jax.sharding import PartitionSpec as P

D = 7168
QR = 1536
KVR = 512
QK_NOPE = 128
V_DIM = 128


def for_sending(shard):
    return jax.tree.map(lambda a: a.astype(jnp.bfloat16) if a.dtype == jnp.float32 else a, shard)


def head_order(owner_map, per_group):
    head_count = owner_map.shape[1]
    head_index = jnp.arange(head_count, dtype=jnp.int32)
    same_owner = owner_map[:, :, None] == owner_map[:, None, :]
    before = head_index[None, None, :] < head_index[None, :, None]
    head_rank = jnp.sum(jnp.logical_and(same_owner, before).astype(jnp.int32), axis=2)
    head_slot = owner_map * per_group + head_rank
    slot_hits = head_slot[:, :, None] == head_index[None, None, :]
    return jnp.sum(jnp.where(slot_hits, head_index[None, :, None], 0), axis=1)


def cut_pieces(local_flat, begins, width_now, granule):
    layer_count, heads_here = begins.shape
    row_table = local_flat.reshape(layer_count, local_flat.shape[1] // granule, granule)
    row_steps = jnp.arange(width_now // granule, dtype=jnp.int32)
    row_ids = (begins[:, :, None] // granule + row_steps[None, None, :]).reshape(
        layer_count, heads_here * (width_now // granule)
    )
    picked = jnp.take_along_axis(row_table, row_ids[:, :, None], axis=1)
    return picked.reshape(layer_count, heads_here, width_now)


def refresh(local_flat, param_offsets, head_at, slice_row):
    fsdp_ways = lax.axis_size("fsdp")
    tensor_ways = lax.axis_size("tp")
    rank_total = fsdp_ways * tensor_ways
    layer_count = local_flat.shape[0]
    per_group = head_at.shape[1] // fsdp_ways
    widths = (
        QR * QK_NOPE // rank_total,
        QK_NOPE * KVR // rank_total,
        V_DIM * KVR // rank_total,
        D * V_DIM // rank_total,
    )
    granule = math.gcd(math.gcd(widths[0], widths[1]), math.gcd(widths[2], widths[3]))
    begins = jnp.take_along_axis(param_offsets, head_at[:, :, None], axis=1)
    pieces = tuple(
        (
            cut_pieces(local_flat, begins[:, :, kind_id], widths[kind_id], granule).reshape(
                layer_count, fsdp_ways, per_group, 1, widths[kind_id]
            )
            for kind_id in range(4)
        )
    )
    arrived = jax.tree.map(
        lambda part, own: part.astype(own.dtype),
        lax.all_to_all(for_sending(pieces), "fsdp", split_axis=1, concat_axis=3, tiled=True),
        pieces,
    )
    query_part, key_part, value_part, out_part = tuple(
        (
            arrived[kind_id].reshape(layer_count, per_group, fsdp_ways, 1, widths[kind_id])
            for kind_id in range(4)
        )
    )
    slice_query = QR // tensor_ways
    slice_output = D // tensor_ways
    blocks = fsdp_ways // tensor_ways

    def to_send(part_in, width_now):
        grouped = part_in.reshape(layer_count, per_group, tensor_ways, blocks, width_now)
        return jnp.take(grouped, slice_row, axis=2).reshape(
            layer_count, per_group, tensor_ways, blocks, 1, width_now
        )

    query_rows, out_rows = (
        lax.all_to_all(
            to_send(query_part, widths[0]), "tp", split_axis=2, concat_axis=4, tiled=True
        ),
        lax.all_to_all(to_send(out_part, widths[3]), "tp", split_axis=2, concat_axis=4, tiled=True),
    )
    query_rows = query_rows.reshape(layer_count, per_group, slice_query, QK_NOPE)
    out_rows = out_rows.reshape(layer_count, per_group, slice_output, V_DIM)
    key_full, value_full = (
        lax.all_gather(key_part, "tp", axis=3, tiled=True),
        lax.all_gather(value_part, "tp", axis=3, tiled=True),
    )
    key_full = key_full.reshape(layer_count, per_group, QK_NOPE, KVR)
    value_full = value_full.reshape(layer_count, per_group, V_DIM, KVR)
    query_absorbed = jnp.einsum(
        "lhrc,lhck->lhrk", query_rows, key_full, preferred_element_type=jnp.float32
    ).astype(jnp.bfloat16)
    output_absorbed = jnp.einsum(
        "lhrc,lhck->lhrk", out_rows, value_full, preferred_element_type=jnp.float32
    ).astype(jnp.bfloat16)
    return (query_absorbed, output_absorbed)


def per_device(learner_flat, param_offsets, owner_map, slice_map):
    fsdp_ways = lax.axis_size("fsdp")
    per_group = owner_map.shape[1] // fsdp_ways
    head_at = head_order(owner_map, per_group)
    slice_row = lax.dynamic_index_in_dim(slice_map, lax.axis_index("fsdp"), 0, keepdims=False)
    layer_results = [
        refresh(
            learner_flat[layer_id : layer_id + 1],
            param_offsets[layer_id : layer_id + 1],
            head_at[layer_id : layer_id + 1],
            slice_row,
        )
        for layer_id in range(learner_flat.shape[0])
    ]
    query_absorbed = jnp.concatenate([result_pair[0] for result_pair in layer_results], axis=0)
    output_absorbed = jnp.concatenate([result_pair[1] for result_pair in layer_results], axis=0)
    return (query_absorbed, output_absorbed)


def solution(mesh):
    placed = (P(None, ("fsdp", "tp")), P(), P(), P())
    return jax.shard_map(
        per_device,
        mesh=mesh,
        in_specs=placed,
        out_specs=(P(None, "fsdp", "tp", None), P(None, "fsdp", "tp", None)),
        check_vma=False,
    )
```

profile of v0, /device:TPU:38, one launch (start us, length us, event | category | flops | bytes accessed | tf_op | source)
XLA Modules:
  0.0 371.7 jit_solution(2697430013469942218)
XLA Ops:
  0.7 0.9 convert_reduce_fusion
  4.4 28.8 %slice_reduce_fusion.1 = (bf16[622592]{0:T(1024)(128)(2,1)S(1)}, bf16[622592]{0:T(1024)(128)(2,1)}) fusion(bf16[2,622592]{1,0:T(2,128)(2,1)} %param.16), kind=kLoop, calls=%fused_computation.18 | loop fusion | bytes 4980736 | tf_op jit(solution)/shard_map/slice | solution.py:113
  33.6 0.8 gather_fusion.10
  35.2 7.6 %all-to-all-start.8 = ((bf16[1,32,4,1,256]{4,2,3,0,1:T(4,128)(2,1)}), bf16[1,32,4,1,256]{4,2,3,0,1:T(4,128)(2,1)S(1)}, u32[]{:S(2)}, u32[]{:S(2)}) async-start(bf16[1,32,4,1,256]{4,2,3,0,1:T(4,128)(2,1)} %bitcast.57), calls=%async_computation.8 | async-start | bytes 131072 | tf_op jit(solution)/shard_map/all_to_all | solution.py:64
  46.0 0.9 gather_fusion.3
  46.9 2.1 gather_fusion.1
  48.9 2.2 reshape.662
  51.2 0.8 gather_fusion.13
  52.0 0.8 gather_fusion.7
  53.0 0.8 bitcast_select_fusion.7
  55.8 7.4 %all-to-all-start.2 = ((bf16[1,32,4,1,256]{4,2,3,0,1:T(4,128)(2,1)}), bf16[1,32,4,1,256]{4,2,3,0,1:T(4,128)(2,1)S(1)}, u32[]{:S(2)}, u32[]{:S(2)}) async-start(bf16[1,32,4,1,256]{4,2,3,0,1:T(4,128)(2,1)} %bitcast.18), calls=%async_computation.2 | async-start | bytes 131072 | tf_op jit(solution)/shard_map/all_to_all | solution.py:64
  63.2 1.2 and_reduce_fusion.5
  65.1 3.8 %all-to-all-done.2 = bf16[1,32,4,1,256]{4,2,3,0,1:T(4,128)(2,1)S(1)} async-done(((bf16[1,32,4,1,256]{4,2,3,0,1:T(4,128)(2,1)}), bf16[1,32,4,1,256]{4,2,3,0,1:T(4,128)(2,1)S(1)}, u32[]{:S(2)}, u32[]{:S(2)}) %all-to-all-start.2) | async-done | bytes 65568 | tf_op jit(solution)/shard_map/all_to_all | solution.py:64
  68.9 6.2 %all-to-all-start.11 = ((bf16[1,32,4,1,256]{4,2,3,0,1:T(4,128)(2,1)}), bf16[1,32,4,1,256]{4,2,3,0,1:T(4,128)(2,1)}, u32[]{:S(2)}, u32[]{:S(2)}) async-start(bf16[1,32,4,1,256]{4,2,3,0,1:T(4,128)(2,1)} %bitcast.74), calls=%async_computation.11 | async-start | bytes 131072 | tf_op jit(solution)/shard_map/all_to_all | solution.py:64
  75.1 5.5 %gather_fusion.8 = bf16[1792,256]{1,0:T(8,128)(2,1)S(1)} fusion(bf16[2432,256]{1,0:T(8,128)(2,1)S(1)} %reshape.643, s32[2048]{0:T(1024)S(1)} %pad_clamp_fusion.1), kind=kCustom, calls=%fused_computation.4.clone | custom fusion | bytes 1842176 | tf_op jit(solution)/shard_map/jit(take_along_axis)/gather | solution.py:36
  80.6 1.7 reshape_reshape.24
  82.3 1.5 reshape.457
  83.8 7.5 %all-to-all-start.5 = ((bf16[1,32,4,1,256]{4,2,3,0,1:T(4,128)(2,1)}), bf16[1,32,4,1,256]{4,2,3,0,1:T(4,128)(2,1)S(1)}, u32[]{:S(2)}, u32[]{:S(2)}) async-start(bf16[1,32,4,1,256]{4,2,3,0,1:T(4,128)(2,1)} %bitcast.40), calls=%async_computation.5 | async-start | bytes 131072 | tf_op jit(solution)/shard_map/all_to_all | solution.py:64
  91.3 2.1 gather_fusion.5
  93.4 3.6 all-to-all-done.5
  97.6 5.6 %all-to-all-start = ((bf16[1,32,4,1,768]{4,2,3,0,1:T(4,128)(2,1)}), bf16[1,32,4,1,768]{4,2,3,0,1:T(4,128)(2,1)S(1)}, u32[]{:S(2)}, u32[]{:S(2)}) async-start(bf16[1,32,4,1,768]{4,2,3,0,1:T(4,128)(2,1)} %bitcast.6), calls=%async_computation | async-start | bytes 393216 | tf_op jit(solution)/shard_map/all_to_all | solution.py:64
  103.3 0.8 reshape_reshape.26
  104.1 5.7 %all-to-all-done = bf16[1,32,4,1,768]{4,2,3,0,1:T(4,128)(2,1)S(1)} async-done(((bf16[1,32,4,1,768]{4,2,3,0,1:T(4,128)(2,1)}), bf16[1,32,4,1,768]{4,2,3,0,1:T(4,128)(2,1)S(1)}, u32[]{:S(2)}, u32[]{:S(2)}) %all-to-all-start) | async-done | bytes 196640 | tf_op jit(solution)/shard_map/all_to_all | solution.py:64
  109.8 5.5 %all-to-all-start.3 = ((bf16[1,32,4,1,768]{4,2,3,0,1:T(4,128)(2,1)}), bf16[1,32,4,1,768]{4,2,3,0,1:T(4,128)(2,1)S(1)}, u32[]{:S(2)}, u32[]{:S(2)}) async-start(bf16[1,32,4,1,768]{4,2,3,0,1:T(4,128)(2,1)} %bitcast.28), calls=%async_computation.3 | async-start | bytes 393216 | tf_op jit(solution)/shard_map/all_to_all | solution.py:64
  115.6 1.3 reshape_reshape.28
  116.9 4.9 %all-to-all-done.3 = bf16[1,32,4,1,768]{4,2,3,0,1:T(4,128)(2,1)S(1)} async-done(((bf16[1,32,4,1,768]{4,2,3,0,1:T(4,128)(2,1)}), bf16[1,32,4,1,768]{4,2,3,0,1:T(4,128)(2,1)S(1)}, u32[]{:S(2)}, u32[]{:S(2)}) %all-to-all-start.3) | async-done | bytes 196640 | tf_op jit(solution)/shard_map/all_to_all | solution.py:64
  121.9 5.5 %all-to-all-start.6 = ((bf16[1,32,4,1,3584]{4,2,3,0,1:T(4,128)(2,1)}), bf16[1,32,4,1,3584]{4,2,3,0,1:T(4,128)(2,1)S(1)}, u32[]{:S(2)}, u32[]{:S(2)}) async-start(bf16[1,32,4,1,3584]{4,2,3,0,1:T(4,128)(2,1)} %bitcast.45), calls=%async_computation.6 | async-start | bytes 1835008 | tf_op jit(solution)/shard_map/all_to_all | solution.py:64
  127.4 5.5 %gather_fusion.11 = bf16[1792,256]{1,0:T(8,128)(2,1)S(1)} fusion(bf16[2432,256]{1,0:T(8,128)(2,1)S(1)} %reshape.662, s32[2048]{0:T(1024)S(1)} %pad_clamp_fusion), kind=kCustom, calls=%fused_computation.12.clone | custom fusion | bytes 1842176 | tf_op jit(solution)/shard_map/jit(take_along_axis)/gather | solution.py:36
  133.2 1.3 reshape_reshape.30
  134.5 6.2 %all-to-all-done.6 = bf16[1,32,4,1,3584]{4,2,3,0,1:T(4,128)(2,1)S(1)} async-done(((bf16[1,32,4,1,3584]{4,2,3,0,1:T(4,128)(2,1)}), bf16[1,32,4,1,3584]{4,2,3,0,1:T(4,128)(2,1)S(1)}, u32[]{:S(2)}, u32[]{:S(2)}) %all-to-all-start.6) | async-done | bytes 917536 | tf_op jit(solution)/shard_map/all_to_all | solution.py:64
  140.7 6.4 %all-to-all-start.9 = ((bf16[1,32,4,1,3584]{4,2,3,0,1:T(4,128)(2,1)}), bf16[1,32,4,1,3584]{4,2,3,0,1:T(4,128)(2,1)S(1)}, u32[]{:S(2)}, u32[]{:S(2)}) async-start(bf16[1,32,4,1,3584]{4,2,3,0,1:T(4,128)(2,1)} %bitcast.62), calls=%async_computation.9 | async-start | bytes 1835008 | tf_op jit(solution)/shard_map/all_to_all | solution.py:64
  147.5 0.7 gather_fusion.2
  148.2 0.7 gather_fusion.6
  149.0 1.0 fusion.5
  149.9 10.5 %all-to-all-done.9 = bf16[1,32,4,1,3584]{4,2,3,0,1:T(4,128)(2,1)S(1)} async-done(((bf16[1,32,4,1,3584]{4,2,3,0,1:T(4,128)(2,1)}), bf16[1,32,4,1,3584]{4,2,3,0,1:T(4,128)(2,1)S(1)}, u32[]{:S(2)}, u32[]{:S(2)}) %all-to-all-start.9) | async-done | bytes 917536 | tf_op jit(solution)/shard_map/all_to_all | solution.py:64
  160.4 8.6 %all-to-all-start.1 = ((bf16[1,4,8,4,1,768]{5,3,1,4,0,2:T(4,128)(2,1)}), bf16[1,4,8,4,1,768]{5,3,1,4,0,2:T(4,128)(2,1)S(1)}, u32[]{:S(2)}, u32[]{:S(2)}) async-start(bf16[1,4,8,4,1,768]{5,3,1,4,0,2:T(4,128)(2,1)} %get-tuple-element.46), calls=%async_computation.1 | async-start | bytes 393216 | tf_op jit(solution)/shard_map/all_to_all | solution.py:84
  169.4 1.3 gather_fusion.9
  171.1 1.3 gather_fusion.12
  172.4 7.0 %all-to-all-done.1 = bf16[1,4,8,4,1,768]{5,3,1,4,0,2:T(4,128)(2,1)S(1)} async-done(((bf16[1,4,8,4,1,768]{5,3,1,4,0,2:T(4,128)(2,1)}), bf16[1,4,8,4,1,768]{5,3,1,4,0,2:T(4,128)(2,1)S(1)}, u32[]{:S(2)}, u32[]{:S(2)}) %all-to-all-start.1) | async-done | bytes 196640 | tf_op jit(solution)/shard_map/all_to_all | solution.py:84
  179.4 4.8 %all-to-all-start.4 = ((bf16[1,4,8,4,1,768]{5,3,1,4,0,2:T(4,128)(2,1)}), bf16[1,4,8,4,1,768]{5,3,1,4,0,2:T(4,128)(2,1)S(1)}, u32[]{:S(2)}, u32[]{:S(2)}) async-start(bf16[1,4,8,4,1,768]{5,3,1,4,0,2:T(4,128)(2,1)} %get-tuple-element.47), calls=%async_computation.4 | async-start | bytes 393216 | tf_op jit(solution)/shard_map/all_to_all | solution.py:84
  184.2 1.8 fusion.3
  186.0 7.8 %all-to-all-done.4 = bf16[1,4,8,4,1,768]{5,3,1,4,0,2:T(4,128)(2,1)S(1)} async-done(((bf16[1,4,8,4,1,768]{5,3,1,4,0,2:T(4,128)(2,1)}), bf16[1,4,8,4,1,768]{5,3,1,4,0,2:T(4,128)(2,1)S(1)}, u32[]{:S(2)}, u32[]{:S(2)}) %all-to-all-start.4) | async-done | bytes 196640 | tf_op jit(solution)/shard_map/all_to_all | solution.py:84
  193.8 27.8 %all_to_all.180 = bf16[1,4,8,4,1,3584]{5,3,1,4,0,2:T(4,128)(2,1)S(1)} all-to-all(bf16[1,4,8,4,1,3584]{5,3,1,4,0,2:T(4,128)(2,1)S(1)} %get-tuple-element.44), channel_id=1, replica_groups=mesh['fsdp'=32,'tp'=8] {'tp'}, dimensions={2} | all-to-all | bytes 1835008 | tf_op jit(solution)/shard_map/all_to_all | solution.py:87
  221.6 4.9 %all-to-all-start.10 = ((bf16[1,4,8,4,1,3584]{5,3,1,4,0,2:T(4,128)(2,1)}), bf16[1,4,8,4,1,3584]{5,3,1,4,0,2:T(4,128)(2,1)S(1)}, u32[]{:S(2)}, u32[]{:S(2)}) async-start(bf16[1,4,8,4,1,3584]{5,3,1,4,0,2:T(4,128)(2,1)} %get-tuple-element.45), calls=%async_computation.10 | async-start | bytes 1835008 | tf_op jit(solution)/shard_map/all_to_all | solution.py:87
  226.5 41.6 %all-gather = bf16[1,1,4,32,8,256]{5,3,4,2,1,0:T(8,128)(2,1)S(1)} all-gather(bf16[1,1,4,32,1,256]{5,3,4,2,1,0:T(8,128)(2,1)S(1)} %bitcast.216), channel_id=2, replica_groups=mesh['fsdp'=32,'tp'=8] {'tp'}, dimensions={4}, use_global_device_ids=true | all-gather | bytes 589824 | tf_op jit(solution)/shard_map/all_gather | solution.py:92
  268.6 25.5 %all-gather.2 = bf16[1,1,4,32,8,256]{5,3,4,2,1,0:T(8,128)(2,1)S(1)} all-gather(bf16[1,1,4,32,1,256]{5,3,4,2,1,0:T(8,128)(2,1)S(1)} %bitcast.217), channel_id=4, replica_groups=mesh['fsdp'=32,'tp'=8] {'tp'}, dimensions={4}, use_global_device_ids=true | all-gather | bytes 589824 | tf_op jit(solution)/shard_map/all_gather | solution.py:93
  294.6 25.5 %all-gather.1 = bf16[1,1,4,32,8,256]{5,3,4,2,1,0:T(8,128)(2,1)S(1)} all-gather(bf16[1,1,4,32,1,256]{5,3,4,2,1,0:T(8,128)(2,1)S(1)} %bitcast.218), channel_id=3, replica_groups=mesh['fsdp'=32,'tp'=8] {'tp'}, dimensions={4}, use_global_device_ids=true | all-gather | bytes 589824 | tf_op jit(solution)/shard_map/all_gather | solution.py:92
  320.1 1.1 copy.105
  321.2 1.2 reshape.459
  322.4 0.8 copy.138
  323.3 25.2 %all-gather.3 = bf16[1,1,4,32,8,256]{5,3,4,2,1,0:T(8,128)(2,1)S(1)} all-gather(bf16[1,1,4,32,1,256]{5,3,4,2,1,0:T(8,128)(2,1)S(1)} %bitcast.219), channel_id=5, replica_groups=mesh['fsdp'=32,'tp'=8] {'tp'}, dimensions={4}, use_global_device_ids=true | all-gather | bytes 589824 | tf_op jit(solution)/shard_map/all_gather | solution.py:93
  348.5 1.1 copy.119
  349.6 2.0 reshape.469
  351.6 1.7 copy.94
  353.3 1.8 reshape.450
  355.0 1.7 copy.102
  356.7 1.8 reshape.456
  358.5 1.3 fusion
  360.2 1.3 pad_maximum_fusion.1
  362.0 1.1 reshape.461
  363.7 1.1 reshape.466
  364.8 2.1 convert_bitcast_fusion
  367.0 1.1 convert_bitcast_fusion.1
  368.1 3.7 pad_maximum_fusion
  (106 shorter events, 14.8 us)
Async XLA Ops:
  0.6 146.5 %copy-start = (s32[32,8]{0,1:T(8,128)S(1)}, s32[32,8]{0,1:T(8,128)}, u32[]{:S(2)}) copy-start(s32[32,8]{0,1:T(8,128)} %param.19) | copy-start | bytes 3076
  35.2 20.7 %all-to-all-start.8 = ((bf16[1,32,4,1,256]{4,2,3,0,1:T(4,128)(2,1)}), bf16[1,32,4,1,256]{4,2,3,0,1:T(4,128)(2,1)S(1)}, u32[]{:S(2)}, u32[]{:S(2)}) async-start(bf16[1,32,4,1,256]{4,2,3,0,1:T(4,128)(2,1)} %bitcast.57), calls=%async_computation.8 | async-start | bytes 131072 | tf_op jit(solution)/shard_map/all_to_all | solution.py:64
  55.8 13.1 %all-to-all-start.2 = ((bf16[1,32,4,1,256]{4,2,3,0,1:T(4,128)(2,1)}), bf16[1,32,4,1,256]{4,2,3,0,1:T(4,128)(2,1)S(1)}, u32[]{:S(2)}, u32[]{:S(2)}) async-start(bf16[1,32,4,1,256]{4,2,3,0,1:T(4,128)(2,1)} %bitcast.18), calls=%async_computation.2 | async-start | bytes 131072 | tf_op jit(solution)/shard_map/all_to_all | solution.py:64
  68.9 14.9 %all-to-all-start.11 = ((bf16[1,32,4,1,256]{4,2,3,0,1:T(4,128)(2,1)}), bf16[1,32,4,1,256]{4,2,3,0,1:T(4,128)(2,1)}, u32[]{:S(2)}, u32[]{:S(2)}) async-start(bf16[1,32,4,1,256]{4,2,3,0,1:T(4,128)(2,1)} %bitcast.74), calls=%async_computation.11 | async-start | bytes 131072 | tf_op jit(solution)/shard_map/all_to_all | solution.py:64
  80.6 22.6 %copy-start.13 = (pred[384]{0:T(512)(128)(4,1)S(1)}, pred[384]{0:T(512)(128)(4,1)}, u32[]{:S(2)}) copy-start(pred[384]{0:T(512)(128)(4,1)} %get-tuple-element.38) | copy-start | bytes 1156
  83.8 13.2 %all-to-all-start.5 = ((bf16[1,32,4,1,256]{4,2,3,0,1:T(4,128)(2,1)}), bf16[1,32,4,1,256]{4,2,3,0,1:T(4,128)(2,1)S(1)}, u32[]{:S(2)}, u32[]{:S(2)}) async-start(bf16[1,32,4,1,256]{4,2,3,0,1:T(4,128)(2,1)} %bitcast.40), calls=%async_computation.5 | async-start | bytes 131072 | tf_op jit(solution)/shard_map/all_to_all | solution.py:64
  91.3 24.0 %copy-start.12 = (pred[1792]{0:T(1024)(128)(4,1)S(1)}, pred[1792]{0:T(1024)(128)(4,1)}, u32[]{:S(2)}) copy-start(pred[1792]{0:T(1024)(128)(4,1)} %get-tuple-element.16) | copy-start | bytes 5380
  97.0 0.6 copy-start.8
  97.6 12.2 %all-to-all-start = ((bf16[1,32,4,1,768]{4,2,3,0,1:T(4,128)(2,1)}), bf16[1,32,4,1,768]{4,2,3,0,1:T(4,128)(2,1)S(1)}, u32[]{:S(2)}, u32[]{:S(2)}) async-start(bf16[1,32,4,1,768]{4,2,3,0,1:T(4,128)(2,1)} %bitcast.6), calls=%async_computation | async-start | bytes 393216 | tf_op jit(solution)/shard_map/all_to_all | solution.py:64
  109.8 5.5 %copy-start.1 = (bf16[1,32,4,1,768]{4,2,3,0,1:T(4,128)(2,1)}, bf16[1,32,4,1,768]{4,2,3,0,1:T(4,128)(2,1)S(1)}, u32[]{:S(2)}) copy-start(bf16[1,32,4,1,768]{4,2,3,0,1:T(4,128)(2,1)S(1)} %all-to-all-done) | copy-start | bytes 589828
  109.8 12.1 %all-to-all-start.3 = ((bf16[1,32,4,1,768]{4,2,3,0,1:T(4,128)(2,1)}), bf16[1,32,4,1,768]{4,2,3,0,1:T(4,128)(2,1)S(1)}, u32[]{:S(2)}, u32[]{:S(2)}) async-start(bf16[1,32,4,1,768]{4,2,3,0,1:T(4,128)(2,1)} %bitcast.28), calls=%async_computation.3 | async-start | bytes 393216 | tf_op jit(solution)/shard_map/all_to_all | solution.py:64
  115.6 11.7 %copy-start.10 = (s32[1,1792,1]{1,2,0:T(1,128)S(1)}, s32[1,1792,1]{1,2,0:T(1,128)}, u32[]{:S(2)}) copy-start(s32[1,1792,1]{1,2,0:T(1,128)} %get-tuple-element.35) | copy-start | bytes 21508
  121.9 11.0 %copy-start.4 = (bf16[1,32,4,1,768]{4,2,3,0,1:T(4,128)(2,1)}, bf16[1,32,4,1,768]{4,2,3,0,1:T(4,128)(2,1)S(1)}, u32[]{:S(2)}) copy-start(bf16[1,32,4,1,768]{4,2,3,0,1:T(4,128)(2,1)S(1)} %all-to-all-done.3) | copy-start | bytes 589828
  121.9 18.8 %all-to-all-start.6 = ((bf16[1,32,4,1,3584]{4,2,3,0,1:T(4,128)(2,1)}), bf16[1,32,4,1,3584]{4,2,3,0,1:T(4,128)(2,1)S(1)}, u32[]{:S(2)}, u32[]{:S(2)}) async-start(bf16[1,32,4,1,3584]{4,2,3,0,1:T(4,128)(2,1)} %bitcast.45), calls=%async_computation.6 | async-start | bytes 1835008 | tf_op jit(solution)/shard_map/all_to_all | solution.py:64
  127.4 5.5 %copy-start.11 = (pred[1792]{0:T(1024)(128)(4,1)S(1)}, pred[1792]{0:T(1024)(128)(4,1)}, u32[]{:S(2)}) copy-start(pred[1792]{0:T(1024)(128)(4,1)} %get-tuple-element.34) | copy-start | bytes 5380
  133.2 14.1 %copy-start.2 = (bf16[1,32,4,1,768]{4,2,3,0,1:T(4,128)(2,1)S(1)}, bf16[1,32,4,1,768]{4,2,3,0,1:T(4,128)(2,1)}, u32[]{:S(2)}) copy-start(bf16[1,32,4,1,768]{4,2,3,0,1:T(4,128)(2,1)} %copy-done.1) | copy-start | bytes 589828
  134.5 12.9 %copy-start.5 = (bf16[1,32,4,1,768]{4,2,3,0,1:T(4,128)(2,1)S(1)}, bf16[1,32,4,1,768]{4,2,3,0,1:T(4,128)(2,1)}, u32[]{:S(2)}) copy-start(bf16[1,32,4,1,768]{4,2,3,0,1:T(4,128)(2,1)} %copy-done.4) | copy-start | bytes 589828
  140.7 19.8 %all-to-all-start.9 = ((bf16[1,32,4,1,3584]{4,2,3,0,1:T(4,128)(2,1)}), bf16[1,32,4,1,3584]{4,2,3,0,1:T(4,128)(2,1)S(1)}, u32[]{:S(2)}, u32[]{:S(2)}) async-start(bf16[1,32,4,1,3584]{4,2,3,0,1:T(4,128)(2,1)} %bitcast.62), calls=%async_computation.9 | async-start | bytes 1835008 | tf_op jit(solution)/shard_map/all_to_all | solution.py:64
  160.4 19.0 %all-to-all-start.1 = ((bf16[1,4,8,4,1,768]{5,3,1,4,0,2:T(4,128)(2,1)}), bf16[1,4,8,4,1,768]{5,3,1,4,0,2:T(4,128)(2,1)S(1)}, u32[]{:S(2)}, u32[]{:S(2)}) async-start(bf16[1,4,8,4,1,768]{5,3,1,4,0,2:T(4,128)(2,1)} %get-tuple-element.46), calls=%async_computation.1 | async-start | bytes 393216 | tf_op jit(solution)/shard_map/all_to_all | solution.py:84
  179.4 6.6 %copy-start.3 = (bf16[1,4,8,4,1,768]{5,3,1,4,0,2:T(4,128)(2,1)}, bf16[1,4,8,4,1,768]{5,3,1,4,0,2:T(4,128)(2,1)S(1)}, u32[]{:S(2)}) copy-start(bf16[1,4,8,4,1,768]{5,3,1,4,0,2:T(4,128)(2,1)S(1)} %all-to-all-done.1) | copy-start | bytes 589828
  179.4 14.4 %all-to-all-start.4 = ((bf16[1,4,8,4,1,768]{5,3,1,4,0,2:T(4,128)(2,1)}), bf16[1,4,8,4,1,768]{5,3,1,4,0,2:T(4,128)(2,1)S(1)}, u32[]{:S(2)}, u32[]{:S(2)}) async-start(bf16[1,4,8,4,1,768]{5,3,1,4,0,2:T(4,128)(2,1)} %get-tuple-element.47), calls=%async_computation.4 | async-start | bytes 393216 | tf_op jit(solution)/shard_map/all_to_all | solution.py:84
  193.8 27.8 %copy-start.6 = (bf16[1,4,8,4,1,768]{5,3,1,4,0,2:T(4,128)(2,1)}, bf16[1,4,8,4,1,768]{5,3,1,4,0,2:T(4,128)(2,1)S(1)}, u32[]{:S(2)}) copy-start(bf16[1,4,8,4,1,768]{5,3,1,4,0,2:T(4,128)(2,1)S(1)} %all-to-all-done.4) | copy-start | bytes 589828
  221.6 141.6 %all-to-all-start.10 = ((bf16[1,4,8,4,1,3584]{5,3,1,4,0,2:T(4,128)(2,1)}), bf16[1,4,8,4,1,3584]{5,3,1,4,0,2:T(4,128)(2,1)S(1)}, u32[]{:S(2)}, u32[]{:S(2)}) async-start(bf16[1,4,8,4,1,3584]{5,3,1,4,0,2:T(4,128)(2,1)} %get-tuple-element.45), calls=%async_computation.10 | async-start | bytes 1835008 | tf_op jit(solution)/shard_map/all_to_all | solution.py:87
  268.6 26.0 %copy-start.9 = (bf16[1,32,4,1,256]{4,2,3,0,1:T(4,128)(2,1)S(1)}, bf16[1,32,4,1,256]{4,2,3,0,1:T(4,128)(2,1)}, u32[]{:S(2)}) copy-start(bf16[1,32,4,1,256]{4,2,3,0,1:T(4,128)(2,1)} %copy-done.8) | copy-start | bytes 196612
  358.5 1.3 copy-start.7
where the time goes:
time: 373 us; the launch traced here: 372 us
  blocking collectives  146 us (39%)
  local copies, waits for them, and re-layouts  85.3 us (23%)
  starting transfers between devices  69.7 us (19%)
  waiting for transfers between devices  49.5 us (13%)
  other arithmetic  15.4 us (4%)
  matrix products  4.9 us (1%)
    all_gather x2, blocking collectives, refresh(): lax.all_gather(key_part, 'tp', axis=3, tiled=True)  67.1 us
    all_to_all x8, starting transfers between devices, refresh(): lax.all_to_all(for_sending(pieces), 'fsdp', split_axis=1, concat_axis=3,...  51.5 us
    all_gather x2, blocking collectives, refresh(): lax.all_gather(value_part, 'tp', axis=3, tiled=True)  50.7 us
    all_to_all x8, waiting for transfers between devices, refresh(): lax.all_to_all(for_sending(pieces), 'fsdp', split_axis=1, concat_axis=3,...  34.7 us
    slice x1, local copies, waits for them, and re-layouts, per_device(): learner_flat[layer_id:layer_id + 1]  28.8 us
    all_to_all x1, blocking collectives, refresh(): lax.all_to_all(to_send(out_part, widths[3]), 'tp', split_axis=2, concat_a...  27.8 us
    gather x8, local copies, waits for them, and re-layouts, cut_pieces(): picked = jnp.take_along_axis(row_table, row_ids[:, :, None], axis=1)  18.4 us
    all_to_all x2, waiting for transfers between devices, refresh(): lax.all_to_all(to_send(query_part, widths[0]), 'tp', split_axis=2, concat...  14.8 us
  transfers between devices with their start and end apart: 11, of which 8 were waited for; matrix products, arithmetic and copies ran while one was open for 17% of the time, Pallas kernels for 0%

commit v1 on v0

--- a/solution.py
+++ b/solution.py
@@ -3,12 +3,25 @@
 import jax.numpy as jnp
 from jax import lax
 from jax.sharding import PartitionSpec as P
+from jax.lax import all_to_all, axis_size
 
 D = 7168
 QR = 1536
 KVR = 512
 QK_NOPE = 128
 V_DIM = 128
+
+
+def bring_the_scenes(array_axis, row_axis, patch):
+    return jnp.concatenate(
+        all_to_all(
+            jnp.stack([patch for _ in range(axis_size(row_axis))], axis=0),
+            axis_name=row_axis,
+            split_axis=0,
+            concat_axis=0,
+        ),
+        axis=array_axis,
+    )
 
 
 def for_sending(shard):
@@ -90,7 +103,7 @@
     out_rows = out_rows.reshape(layer_count, per_group, slice_output, V_DIM)
     key_full, value_full = (
         lax.all_gather(key_part, "tp", axis=3, tiled=True),
-        lax.all_gather(value_part, "tp", axis=3, tiled=True),
+        bring_the_scenes(3, "tp", value_part),
     )
     key_full = key_full.reshape(layer_count, per_group, QK_NOPE, KVR)
     value_full = value_full.reshape(layer_count, per_group, V_DIM, KVR)

time: 373 us -> 361 us (0.968)
  blocking collectives: 146 us -> 97 us
  waiting for transfers between devices: 49.5 us -> 81.4 us
  starting transfers between devices: 69.7 us -> 79.1 us
  local copies, waits for them, and re-layouts: 85.3 us -> 80 us
    all_gather x2 -> x0, blocking collectives: 50.7 us -> none  [refresh(): lax.all_gather(value_part, 'tp', axis=3, tiled=True)]
    all_to_all x0 -> x2, waiting for transfers between devices: none -> 28.8 us  [bring_the_scenes(): all_to_all(jnp.stack([patch for _ in range(axis_size(row_axis))], axis=0)...]
    all_to_all x0 -> x2, starting transfers between devices: none -> 11.2 us  [bring_the_scenes(): all_to_all(jnp.stack([patch for _ in range(axis_size(row_axis))], axis=0)...]
    all_to_all x8, waiting for transfers between devices: 34.7 us -> 44.2 us  [refresh(): lax.all_to_all(for_sending(pieces), 'fsdp', split_axis=1, concat_axis=3,...]
    all_to_all x2, waiting for transfers between devices: 14.8 us -> 8.47 us  [refresh(): lax.all_to_all(to_send(query_part, widths[0]), 'tp', split_axis=2, concat...]
    another operation x8 -> x12, local copies, waits for them, and re-layouts: 9.43 us -> 8.41 us
  transfers between devices with their start and end apart: 11 -> 13, of which waited for: 8 -> 11; matrix products, arithmetic and copies ran while one was open for 17% -> 15% of each run, Pallas kernels for 0% -> 0%
where the time goes in v1:
time: 361 us; the launch traced here: 358 us
  blocking collectives  97 us (27%)
  waiting for transfers between devices  81.4 us (23%)
  local copies, waits for them, and re-layouts  80 us (22%)
  starting transfers between devices  79.1 us (22%)
  other arithmetic  14.3 us (4%)
  matrix products  4.92 us (1%)
    all_gather x2, blocking collectives, refresh(): lax.all_gather(key_part, 'tp', axis=3, tiled=True)  68 us
    all_to_all x8, starting transfers between devices, refresh(): lax.all_to_all(for_sending(pieces), 'fsdp', split_axis=1, concat_axis=3,...  49.2 us
    all_to_all x8, waiting for transfers between devices, refresh(): lax.all_to_all(for_sending(pieces), 'fsdp', split_axis=1, concat_axis=3,...  44.2 us
    all_to_all x1, blocking collectives, refresh(): lax.all_to_all(to_send(out_part, widths[3]), 'tp', split_axis=2, concat_a...  29 us
    slice x1, local copies, waits for them, and re-layouts, per_device(): learner_flat[layer_id:layer_id + 1]  28.8 us
    all_to_all x2, waiting for transfers between devices, bring_the_scenes(): all_to_all(jnp.stack([patch for _ in range(axis_size(row_axis))], axis=0)...  28.8 us
    gather x8, local copies, waits for them, and re-layouts, cut_pieces(): picked = jnp.take_along_axis(row_table, row_ids[:, :, None], axis=1)  18.4 us
    all_to_all x2, starting transfers between devices, refresh(): lax.all_to_all(to_send(query_part, widths[0]), 'tp', split_axis=2, concat...  13.8 us
  transfers between devices with their start and end apart: 13, of which 11 were waited for; matrix products, arithmetic and copies ran while one was open for 15% of the time, Pallas kernels for 0%

profile of v1, /device:TPU:38, one launch (start us, length us, event | category | flops | bytes accessed | tf_op | source)
XLA Modules:
  0.0 358.0 jit_solution(1798388790356269182)
XLA Ops:
  0.7 0.9 convert_reduce_fusion
  4.4 28.8 %slice_reduce_fusion.1 = (bf16[622592]{0:T(1024)(128)(2,1)S(1)}, bf16[622592]{0:T(1024)(128)(2,1)}) fusion(bf16[2,622592]{1,0:T(2,128)(2,1)} %param.16), kind=kLoop, calls=%fused_computation.18 | loop fusion | bytes 4980736 | tf_op jit(solution)/shard_map/slice | solution.py:126
  33.6 0.8 gather_fusion.10
  35.2 7.6 %all-to-all-start.8 = ((bf16[1,32,4,1,256]{4,2,3,0,1:T(4,128)(2,1)}), bf16[1,32,4,1,256]{4,2,3,0,1:T(4,128)(2,1)S(1)}, u32[]{:S(2)}, u32[]{:S(2)}) async-start(bf16[1,32,4,1,256]{4,2,3,0,1:T(4,128)(2,1)} %bitcast.57), calls=%async_computation.8 | async-start | bytes 131072 | tf_op jit(solution)/shard_map/all_to_all | solution.py:77
  45.5 0.9 gather_fusion.3
  47.1 2.0 gather_fusion.1
  49.2 2.2 reshape.662
  51.4 0.8 gather_fusion.13
  52.3 2.1 gather_fusion.5
  54.7 0.8 gather_fusion.7
  55.6 7.4 %all-to-all-start.2 = ((bf16[1,32,4,1,256]{4,2,3,0,1:T(4,128)(2,1)}), bf16[1,32,4,1,256]{4,2,3,0,1:T(4,128)(2,1)S(1)}, u32[]{:S(2)}, u32[]{:S(2)}) async-start(bf16[1,32,4,1,256]{4,2,3,0,1:T(4,128)(2,1)} %bitcast.18), calls=%async_computation.2 | async-start | bytes 131072 | tf_op jit(solution)/shard_map/all_to_all | solution.py:77
  63.1 0.8 reshape_reshape.26
  66.1 2.6 all-to-all-done.2
  68.7 5.6 %all-to-all-start = ((bf16[1,32,4,1,768]{4,2,3,0,1:T(4,128)(2,1)}), bf16[1,32,4,1,768]{4,2,3,0,1:T(4,128)(2,1)S(1)}, u32[]{:S(2)}, u32[]{:S(2)}) async-start(bf16[1,32,4,1,768]{4,2,3,0,1:T(4,128)(2,1)} %bitcast.6), calls=%async_computation | async-start | bytes 393216 | tf_op jit(solution)/shard_map/all_to_all | solution.py:77
  74.3 6.6 %all-to-all-done = bf16[1,32,4,1,768]{4,2,3,0,1:T(4,128)(2,1)S(1)} async-done(((bf16[1,32,4,1,768]{4,2,3,0,1:T(4,128)(2,1)}), bf16[1,32,4,1,768]{4,2,3,0,1:T(4,128)(2,1)S(1)}, u32[]{:S(2)}, u32[]{:S(2)}) %all-to-all-start) | async-done | bytes 196640 | tf_op jit(solution)/shard_map/all_to_all | solution.py:77
  80.9 5.5 %all-to-all-start.3 = ((bf16[1,32,4,1,768]{4,2,3,0,1:T(4,128)(2,1)}), bf16[1,32,4,1,768]{4,2,3,0,1:T(4,128)(2,1)S(1)}, u32[]{:S(2)}, u32[]{:S(2)}) async-start(bf16[1,32,4,1,768]{4,2,3,0,1:T(4,128)(2,1)} %bitcast.28), calls=%async_computation.3 | async-start | bytes 393216 | tf_op jit(solution)/shard_map/all_to_all | solution.py:77
  86.4 6.6 %all-to-all-done.3 = bf16[1,32,4,1,768]{4,2,3,0,1:T(4,128)(2,1)S(1)} async-done(((bf16[1,32,4,1,768]{4,2,3,0,1:T(4,128)(2,1)}), bf16[1,32,4,1,768]{4,2,3,0,1:T(4,128)(2,1)S(1)}, u32[]{:S(2)}, u32[]{:S(2)}) %all-to-all-start.3) | async-done | bytes 196640 | tf_op jit(solution)/shard_map/all_to_all | solution.py:77
  92.9 5.5 %all-to-all-start.12 = ((bf16[1,32,4,1,256]{4,2,3,0,1:T(4,128)(2,1)}), bf16[1,32,4,1,256]{4,2,3,0,1:T(4,128)(2,1)S(1)}, u32[]{:S(2)}, u32[]{:S(2)}) async-start(bf16[1,32,4,1,256]{4,2,3,0,1:T(4,128)(2,1)} %bitcast.76), calls=%async_computation.12 | async-start | bytes 131072 | tf_op jit(solution)/shard_map/all_to_all | solution.py:77
  100.1 4.1 %all-to-all-done.12 = bf16[1,32,4,1,256]{4,2,3,0,1:T(4,128)(2,1)S(1)} async-done(((bf16[1,32,4,1,256]{4,2,3,0,1:T(4,128)(2,1)}), bf16[1,32,4,1,256]{4,2,3,0,1:T(4,128)(2,1)S(1)}, u32[]{:S(2)}, u32[]{:S(2)}) %all-to-all-start.12) | async-done | bytes 65568 | tf_op jit(solution)/shard_map/all_to_all | solution.py:77
  104.1 5.6 %all-to-all-start.5 = ((bf16[1,32,4,1,256]{4,2,3,0,1:T(4,128)(2,1)}), bf16[1,32,4,1,256]{4,2,3,0,1:T(4,128)(2,1)S(1)}, u32[]{:S(2)}, u32[]{:S(2)}) async-start(bf16[1,32,4,1,256]{4,2,3,0,1:T(4,128)(2,1)} %bitcast.40), calls=%async_computation.5 | async-start | bytes 131072 | tf_op jit(solution)/shard_map/all_to_all | solution.py:77
  109.7 1.0 fusion.5
  110.7 4.8 %all-to-all-done.5 = bf16[1,32,4,1,256]{4,2,3,0,1:T(4,128)(2,1)S(1)} async-done(((bf16[1,32,4,1,256]{4,2,3,0,1:T(4,128)(2,1)}), bf16[1,32,4,1,256]{4,2,3,0,1:T(4,128)(2,1)S(1)}, u32[]{:S(2)}, u32[]{:S(2)}) %all-to-all-start.5) | async-done | bytes 65568 | tf_op jit(solution)/shard_map/all_to_all | solution.py:77
  115.5 8.6 %all-to-all-start.1 = ((bf16[1,4,8,4,1,768]{5,3,1,4,0,2:T(4,128)(2,1)}), bf16[1,4,8,4,1,768]{5,3,1,4,0,2:T(4,128)(2,1)}, u32[]{:S(2)}, u32[]{:S(2)}) async-start(bf16[1,4,8,4,1,768]{5,3,1,4,0,2:T(4,128)(2,1)} %get-tuple-element.46), calls=%async_computation.1 | async-start | bytes 393216 | tf_op jit(solution)/shard_map/all_to_all | solution.py:97
  124.7 1.2 and_reduce_fusion.5
  125.9 5.5 %gather_fusion.8 = bf16[1792,256]{1,0:T(8,128)(2,1)S(1)} fusion(bf16[2432,256]{1,0:T(8,128)(2,1)S(1)} %reshape.643, s32[2048]{0:T(1024)S(1)} %pad_clamp_fusion.1), kind=kCustom, calls=%fused_computation.4.clone | custom fusion | bytes 1842176 | tf_op jit(solution)/shard_map/jit(take_along_axis)/gather | solution.py:49
  131.4 2.0 all-to-all-done.1
  133.4 5.2 %all-to-all-start.4 = ((bf16[1,4,8,4,1,768]{5,3,1,4,0,2:T(4,128)(2,1)}), bf16[1,4,8,4,1,768]{5,3,1,4,0,2:T(4,128)(2,1)S(1)}, u32[]{:S(2)}, u32[]{:S(2)}) async-start(bf16[1,4,8,4,1,768]{5,3,1,4,0,2:T(4,128)(2,1)} %get-tuple-element.47), calls=%async_computation.4 | async-start | bytes 393216 | tf_op jit(solution)/shard_map/all_to_all | solution.py:97
  138.6 1.0 bitcast_select_fusion.3
  139.6 1.3 reshape_reshape.30
  140.9 6.4 %all-to-all-done.4 = bf16[1,4,8,4,1,768]{5,3,1,4,0,2:T(4,128)(2,1)S(1)} async-done(((bf16[1,4,8,4,1,768]{5,3,1,4,0,2:T(4,128)(2,1)}), bf16[1,4,8,4,1,768]{5,3,1,4,0,2:T(4,128)(2,1)S(1)}, u32[]{:S(2)}, u32[]{:S(2)}) %all-to-all-start.4) | async-done | bytes 196640 | tf_op jit(solution)/shard_map/all_to_all | solution.py:97
  147.4 5.6 %all-to-all-start.6 = ((bf16[1,32,4,1,3584]{4,2,3,0,1:T(4,128)(2,1)}), bf16[1,32,4,1,3584]{4,2,3,0,1:T(4,128)(2,1)S(1)}, u32[]{:S(2)}, u32[]{:S(2)}) async-start(bf16[1,32,4,1,3584]{4,2,3,0,1:T(4,128)(2,1)} %bitcast.45), calls=%async_computation.6 | async-start | bytes 1835008 | tf_op jit(solution)/shard_map/all_to_all | solution.py:77
  153.1 5.5 %gather_fusion.11 = bf16[1792,256]{1,0:T(8,128)(2,1)S(1)} fusion(bf16[2432,256]{1,0:T(8,128)(2,1)S(1)} %reshape.662, s32[2048]{0:T(1024)S(1)} %pad_clamp_fusion), kind=kCustom, calls=%fused_computation.12.clone | custom fusion | bytes 1842176 | tf_op jit(solution)/shard_map/jit(take_along_axis)/gather | solution.py:49
  158.9 1.3 reshape_reshape.32
  160.2 6.2 %all-to-all-done.6 = bf16[1,32,4,1,3584]{4,2,3,0,1:T(4,128)(2,1)S(1)} async-done(((bf16[1,32,4,1,3584]{4,2,3,0,1:T(4,128)(2,1)}), bf16[1,32,4,1,3584]{4,2,3,0,1:T(4,128)(2,1)S(1)}, u32[]{:S(2)}, u32[]{:S(2)}) %all-to-all-start.6) | async-done | bytes 917536 | tf_op jit(solution)/shard_map/all_to_all | solution.py:77
  166.4 6.5 %all-to-all-start.10 = ((bf16[1,32,4,1,3584]{4,2,3,0,1:T(4,128)(2,1)}), bf16[1,32,4,1,3584]{4,2,3,0,1:T(4,128)(2,1)S(1)}, u32[]{:S(2)}, u32[]{:S(2)}) async-start(bf16[1,32,4,1,3584]{4,2,3,0,1:T(4,128)(2,1)} %bitcast.64), calls=%async_computation.10 | async-start | bytes 1835008 | tf_op jit(solution)/shard_map/all_to_all | solution.py:77
  172.9 13.3 %all-to-all-done.10 = bf16[1,32,4,1,3584]{4,2,3,0,1:T(4,128)(2,1)S(1)} async-done(((bf16[1,32,4,1,3584]{4,2,3,0,1:T(4,128)(2,1)}), bf16[1,32,4,1,3584]{4,2,3,0,1:T(4,128)(2,1)S(1)}, u32[]{:S(2)}, u32[]{:S(2)}) %all-to-all-start.10) | async-done | bytes 917536 | tf_op jit(solution)/shard_map/all_to_all | solution.py:77
  186.3 0.9 stack.6
  187.1 5.5 %all-to-all-start.9 = ((bf16[8,1,4,32,1,256]{5,3,2,4,1,0:T(8,128)(2,1)}), bf16[8,1,4,32,1,256]{5,3,2,4,1,0:T(8,128)(2,1)}, u32[]{:S(2)}, u32[]{:S(2)}) async-start(bf16[8,1,4,32,1,256]{5,3,2,4,1,0:T(8,128)(2,1)} %stack.6), calls=%async_computation.9 | async-start | bytes 1048576 | tf_op jit(solution)/shard_map/all_to_all | solution.py:17
  193.0 1.3 gather_fusion.9
  194.7 1.3 gather_fusion.12
  196.1 13.8 %all-to-all-done.9 = bf16[8,1,4,32,1,256]{5,3,2,4,1,0:T(8,128)(2,1)} async-done(((bf16[8,1,4,32,1,256]{5,3,2,4,1,0:T(8,128)(2,1)}), bf16[8,1,4,32,1,256]{5,3,2,4,1,0:T(8,128)(2,1)}, u32[]{:S(2)}, u32[]{:S(2)}) %all-to-all-start.9) | async-done | bytes 524320 | tf_op jit(solution)/shard_map/all_to_all | solution.py:17
  209.9 0.9 stack.7
  210.7 5.8 %all-to-all-start.13 = ((bf16[8,1,4,32,1,256]{5,3,2,4,1,0:T(8,128)(2,1)}), bf16[8,1,4,32,1,256]{5,3,2,4,1,0:T(8,128)(2,1)}, u32[]{:S(2)}, u32[]{:S(2)}) async-start(bf16[8,1,4,32,1,256]{5,3,2,4,1,0:T(8,128)(2,1)} %stack.7), calls=%async_computation.13 | async-start | bytes 1048576 | tf_op jit(solution)/shard_map/all_to_all | solution.py:17
  216.5 1.8 fusion.3
  218.3 14.9 %all-to-all-done.13 = bf16[8,1,4,32,1,256]{5,3,2,4,1,0:T(8,128)(2,1)} async-done(((bf16[8,1,4,32,1,256]{5,3,2,4,1,0:T(8,128)(2,1)}), bf16[8,1,4,32,1,256]{5,3,2,4,1,0:T(8,128)(2,1)}, u32[]{:S(2)}, u32[]{:S(2)}) %all-to-all-start.13) | async-done | bytes 524320 | tf_op jit(solution)/shard_map/all_to_all | solution.py:17
  233.2 29.0 %all_to_all.190 = bf16[1,4,8,4,1,3584]{5,3,1,4,0,2:T(4,128)(2,1)S(1)} all-to-all(bf16[1,4,8,4,1,3584]{5,3,1,4,0,2:T(4,128)(2,1)S(1)} %get-tuple-element.44), channel_id=1, replica_groups=mesh['fsdp'=32,'tp'=8] {'tp'}, dimensions={2} | all-to-all | bytes 1835008 | tf_op jit(solution)/shard_map/all_to_all | solution.py:100
  262.2 4.9 %all-to-all-start.11 = ((bf16[1,4,8,4,1,3584]{5,3,1,4,0,2:T(4,128)(2,1)}), bf16[1,4,8,4,1,3584]{5,3,1,4,0,2:T(4,128)(2,1)S(1)}, u32[]{:S(2)}, u32[]{:S(2)}) async-start(bf16[1,4,8,4,1,3584]{5,3,1,4,0,2:T(4,128)(2,1)} %get-tuple-element.45), calls=%async_computation.11 | async-start | bytes 1835008 | tf_op jit(solution)/shard_map/all_to_all | solution.py:100
  267.1 42.6 %all-gather = bf16[1,1,4,32,8,256]{5,3,4,2,1,0:T(8,128)(2,1)S(1)} all-gather(bf16[1,1,4,32,1,256]{5,3,4,2,1,0:T(8,128)(2,1)S(1)} %bitcast.221), channel_id=2, replica_groups=mesh['fsdp'=32,'tp'=8] {'tp'}, dimensions={4}, use_global_device_ids=true | all-gather | bytes 589824 | tf_op jit(solution)/shard_map/all_gather | solution.py:105
  310.2 25.4 %all-gather.1 = bf16[1,1,4,32,8,256]{5,3,4,2,1,0:T(8,128)(2,1)S(1)} all-gather(bf16[1,1,4,32,1,256]{5,3,4,2,1,0:T(8,128)(2,1)S(1)} %bitcast.222), channel_id=3, replica_groups=mesh['fsdp'=32,'tp'=8] {'tp'}, dimensions={4}, use_global_device_ids=true | all-gather | bytes 589824 | tf_op jit(solution)/shard_map/all_gather | solution.py:105
  335.7 1.1 copy.103
  336.8 1.2 reshape.463
  338.0 1.0 copy.92
  339.0 0.9 reshape.454
  340.1 1.3 fusion
  341.7 1.3 pad_maximum_fusion.1
  343.0 1.3 copy.110
  344.3 1.0 reshape.468
  345.3 1.3 copy.117
  346.6 1.0 reshape.473
  348.1 1.1 reshape.465
  349.8 1.1 reshape.470
  351.0 2.2 convert_bitcast_fusion
  353.2 1.1 convert_bitcast_fusion.1
  354.3 3.7 %pad_maximum_fusion = bf16[2,4,896,512]{3,2,1,0:T(8,128)(2,1)} fusion(bf16[1,4,896,512]{3,2,1,0:T(8,128)(2,1)S(1)} %convert_bitcast_fusion, bf16[1,4,896,512]{3,2,1,0:T(8,128)(2,1)S(1)} %convert_bitcast_fusion.1), kind=kLoop, calls=%fused_computation.14 | loop fusion | flops 3670016 | bytes 14680064 | tf_op jit(solution)/shard_map/concatenate | solution.py:134
  (102 shorter events, 15.5 us)
Async XLA Ops:
  0.6 65.3 %copy-start = (s32[32,8]{0,1:T(8,128)S(1)}, s32[32,8]{0,1:T(8,128)}, u32[]{:S(2)}) copy-start(s32[32,8]{0,1:T(8,128)} %param.19) | copy-start | bytes 3076
  35.2 20.4 %all-to-all-start.8 = ((bf16[1,32,4,1,256]{4,2,3,0,1:T(4,128)(2,1)}), bf16[1,32,4,1,256]{4,2,3,0,1:T(4,128)(2,1)S(1)}, u32[]{:S(2)}, u32[]{:S(2)}) async-start(bf16[1,32,4,1,256]{4,2,3,0,1:T(4,128)(2,1)} %bitcast.57), calls=%async_computation.8 | async-start | bytes 131072 | tf_op jit(solution)/shard_map/all_to_all | solution.py:77
  55.6 13.1 %all-to-all-start.2 = ((bf16[1,32,4,1,256]{4,2,3,0,1:T(4,128)(2,1)}), bf16[1,32,4,1,256]{4,2,3,0,1:T(4,128)(2,1)S(1)}, u32[]{:S(2)}, u32[]{:S(2)}) async-start(bf16[1,32,4,1,256]{4,2,3,0,1:T(4,128)(2,1)} %bitcast.18), calls=%async_computation.2 | async-start | bytes 131072 | tf_op jit(solution)/shard_map/all_to_all | solution.py:77
  68.7 12.2 %all-to-all-start = ((bf16[1,32,4,1,768]{4,2,3,0,1:T(4,128)(2,1)}), bf16[1,32,4,1,768]{4,2,3,0,1:T(4,128)(2,1)S(1)}, u32[]{:S(2)}, u32[]{:S(2)}) async-start(bf16[1,32,4,1,768]{4,2,3,0,1:T(4,128)(2,1)} %bitcast.6), calls=%async_computation | async-start | bytes 393216 | tf_op jit(solution)/shard_map/all_to_all | solution.py:77
  74.3 41.2 %copy-start.8 = (pred[8]{0:T(512)(128)(4,1)}, pred[8]{0:T(512)(128)(4,1)S(1)}, u32[]{:S(2)}) copy-start(pred[8]{0:T(512)(128)(4,1)S(1)} %compare_and_fusion) | copy-start | bytes 28
  80.9 12.0 %all-to-all-start.3 = ((bf16[1,32,4,1,768]{4,2,3,0,1:T(4,128)(2,1)}), bf16[1,32,4,1,768]{4,2,3,0,1:T(4,128)(2,1)S(1)}, u32[]{:S(2)}, u32[]{:S(2)}) async-start(bf16[1,32,4,1,768]{4,2,3,0,1:T(4,128)(2,1)} %bitcast.28), calls=%async_computation.3 | async-start | bytes 393216 | tf_op jit(solution)/shard_map/all_to_all | solution.py:77
  92.9 11.2 %all-to-all-start.12 = ((bf16[1,32,4,1,256]{4,2,3,0,1:T(4,128)(2,1)}), bf16[1,32,4,1,256]{4,2,3,0,1:T(4,128)(2,1)S(1)}, u32[]{:S(2)}, u32[]{:S(2)}) async-start(bf16[1,32,4,1,256]{4,2,3,0,1:T(4,128)(2,1)} %bitcast.76), calls=%async_computation.12 | async-start | bytes 131072 | tf_op jit(solution)/shard_map/all_to_all | solution.py:77
  104.1 21.8 %copy-start.4 = (bf16[1,32,4,1,256]{4,2,3,0,1:T(4,128)(2,1)}, bf16[1,32,4,1,256]{4,2,3,0,1:T(4,128)(2,1)S(1)}, u32[]{:S(2)}) copy-start(bf16[1,32,4,1,256]{4,2,3,0,1:T(4,128)(2,1)S(1)} %all-to-all-done.12) | copy-start | bytes 196612
  104.1 11.3 %all-to-all-start.5 = ((bf16[1,32,4,1,256]{4,2,3,0,1:T(4,128)(2,1)}), bf16[1,32,4,1,256]{4,2,3,0,1:T(4,128)(2,1)S(1)}, u32[]{:S(2)}, u32[]{:S(2)}) async-start(bf16[1,32,4,1,256]{4,2,3,0,1:T(4,128)(2,1)} %bitcast.40), calls=%async_computation.5 | async-start | bytes 131072 | tf_op jit(solution)/shard_map/all_to_all | solution.py:77
  115.5 10.5 %copy-start.2 = (bf16[1,32,4,1,256]{4,2,3,0,1:T(4,128)(2,1)}, bf16[1,32,4,1,256]{4,2,3,0,1:T(4,128)(2,1)S(1)}, u32[]{:S(2)}) copy-start(bf16[1,32,4,1,256]{4,2,3,0,1:T(4,128)(2,1)S(1)} %all-to-all-done.5) | copy-start | bytes 196612
  115.5 18.0 %all-to-all-start.1 = ((bf16[1,4,8,4,1,768]{5,3,1,4,0,2:T(4,128)(2,1)}), bf16[1,4,8,4,1,768]{5,3,1,4,0,2:T(4,128)(2,1)}, u32[]{:S(2)}, u32[]{:S(2)}) async-start(bf16[1,4,8,4,1,768]{5,3,1,4,0,2:T(4,128)(2,1)} %get-tuple-element.46), calls=%async_computation.1 | async-start | bytes 393216 | tf_op jit(solution)/shard_map/all_to_all | solution.py:97
  133.4 13.9 %all-to-all-start.4 = ((bf16[1,4,8,4,1,768]{5,3,1,4,0,2:T(4,128)(2,1)}), bf16[1,4,8,4,1,768]{5,3,1,4,0,2:T(4,128)(2,1)S(1)}, u32[]{:S(2)}, u32[]{:S(2)}) async-start(bf16[1,4,8,4,1,768]{5,3,1,4,0,2:T(4,128)(2,1)} %get-tuple-element.47), calls=%async_computation.4 | async-start | bytes 393216 | tf_op jit(solution)/shard_map/all_to_all | solution.py:97
  139.6 13.4 %copy-start.6 = (s32[1,1792,1]{1,2,0:T(1,128)S(1)}, s32[1,1792,1]{1,2,0:T(1,128)}, u32[]{:S(2)}) copy-start(s32[1,1792,1]{1,2,0:T(1,128)} %get-tuple-element.35) | copy-start | bytes 21508
  147.4 19.0 %all-to-all-start.6 = ((bf16[1,32,4,1,3584]{4,2,3,0,1:T(4,128)(2,1)}), bf16[1,32,4,1,3584]{4,2,3,0,1:T(4,128)(2,1)S(1)}, u32[]{:S(2)}, u32[]{:S(2)}) async-start(bf16[1,32,4,1,3584]{4,2,3,0,1:T(4,128)(2,1)} %bitcast.45), calls=%async_computation.6 | async-start | bytes 1835008 | tf_op jit(solution)/shard_map/all_to_all | solution.py:77
  153.1 5.5 %copy-start.7 = (pred[1792]{0:T(1024)(128)(4,1)S(1)}, pred[1792]{0:T(1024)(128)(4,1)}, u32[]{:S(2)}) copy-start(pred[1792]{0:T(1024)(128)(4,1)} %get-tuple-element.34) | copy-start | bytes 5380
  166.4 26.2 %copy-start.5 = (bf16[1,32,4,1,256]{4,2,3,0,1:T(4,128)(2,1)S(1)}, bf16[1,32,4,1,256]{4,2,3,0,1:T(4,128)(2,1)}, u32[]{:S(2)}) copy-start(bf16[1,32,4,1,256]{4,2,3,0,1:T(4,128)(2,1)} %copy-done.4) | copy-start | bytes 196612
  166.4 19.9 %all-to-all-start.10 = ((bf16[1,32,4,1,3584]{4,2,3,0,1:T(4,128)(2,1)}), bf16[1,32,4,1,3584]{4,2,3,0,1:T(4,128)(2,1)S(1)}, u32[]{:S(2)}, u32[]{:S(2)}) async-start(bf16[1,32,4,1,3584]{4,2,3,0,1:T(4,128)(2,1)} %bitcast.64), calls=%async_computation.10 | async-start | bytes 1835008 | tf_op jit(solution)/shard_map/all_to_all | solution.py:77
  187.1 22.7 %all-to-all-start.9 = ((bf16[8,1,4,32,1,256]{5,3,2,4,1,0:T(8,128)(2,1)}), bf16[8,1,4,32,1,256]{5,3,2,4,1,0:T(8,128)(2,1)}, u32[]{:S(2)}, u32[]{:S(2)}) async-start(bf16[8,1,4,32,1,256]{5,3,2,4,1,0:T(8,128)(2,1)} %stack.6), calls=%async_computation.9 | async-start | bytes 1048576 | tf_op jit(solution)/shard_map/all_to_all | solution.py:17
  194.7 21.8 %copy-start.9 = (pred[8]{0:T(512)(128)(4,1)S(1)}, pred[8]{0:T(512)(128)(4,1)}, u32[]{:S(2)}) copy-start(pred[8]{0:T(512)(128)(4,1)} %copy-done.8) | copy-start | bytes 28
  210.7 22.5 %all-to-all-start.13 = ((bf16[8,1,4,32,1,256]{5,3,2,4,1,0:T(8,128)(2,1)}), bf16[8,1,4,32,1,256]{5,3,2,4,1,0:T(8,128)(2,1)}, u32[]{:S(2)}, u32[]{:S(2)}) async-start(bf16[8,1,4,32,1,256]{5,3,2,4,1,0:T(8,128)(2,1)} %stack.7), calls=%async_computation.13 | async-start | bytes 1048576 | tf_op jit(solution)/shard_map/all_to_all | solution.py:17
  262.2 87.1 %all-to-all-start.11 = ((bf16[1,4,8,4,1,3584]{5,3,1,4,0,2:T(4,128)(2,1)}), bf16[1,4,8,4,1,3584]{5,3,1,4,0,2:T(4,128)(2,1)S(1)}, u32[]{:S(2)}, u32[]{:S(2)}) async-start(bf16[1,4,8,4,1,3584]{5,3,1,4,0,2:T(4,128)(2,1)} %get-tuple-element.45), calls=%async_computation.11 | async-start | bytes 1835008 | tf_op jit(solution)/shard_map/all_to_all | solution.py:100
  267.1 43.1 %copy-start.3 = (bf16[1,32,4,1,256]{4,2,3,0,1:T(4,128)(2,1)S(1)}, bf16[1,32,4,1,256]{4,2,3,0,1:T(4,128)(2,1)}, u32[]{:S(2)}) copy-start(bf16[1,32,4,1,256]{4,2,3,0,1:T(4,128)(2,1)} %copy-done.2) | copy-start | bytes 196612
  351.0 2.2 copy-start.1
